TPU v7x, 32 devices: a whole 2x2x4 slice. The times are simulated.
32 devices in a mesh: groups: 2 (over y), expert: 4 (over z), tensor: 4 (over x, core), sub: 1.
Axes of the slice: x: 2, y: 2, z: 4, core: 2. Of those that a mesh axis runs over, the one named last changes fastest.
Arguments:
- hidden_rows: bfloat16 [4, 320, 4096], P(None, ('groups', 'expert', 'tensor')), parts along dimension 1, may hold values from -6 to 6
- expert_ids: int32 [4, 320, 8], P(None, ('groups', 'expert', 'tensor')), parts along dimension 1, may hold values from 0 to 15, all different within a row; in each aligned block of 10 rows (0 to 9, 10 to 19, ..., all dimensions but the last counted through in order) at most 5 rows name the same one
- accepted: int32 [4, 64], P(None, ('groups', 'expert', 'tensor')), parts along dimension 1, may hold values from 0 to 4
- norm_gain: float32 [4096], replicated, may hold values from 0.5 to 1.5
- router: bfloat16 [4096, 16], replicated, may hold values from -0.0625 to 0.0625
- gate_weight: bfloat16 [16, 4096, 768], P(('expert', 'tensor'), None, 'sub'), may hold values from -0.09375 to 0.09375
- up_weight: bfloat16 [16, 4096, 768], P(('expert', 'tensor'), None, 'sub'), may hold values from -0.09375 to 0.09375
- down_weight: bfloat16 [16, 768, 4096], P(('expert', 'tensor'), 'sub'), may hold values from -0.21875 to 0.21875
- draft_gain: float32 [4096], replicated, may hold values from 0.5 to 1.5
- draft_gate: bfloat16 [4096, 6144], P(None, ('expert', 'tensor')), may hold values from -0.09375 to 0.09375
- draft_up: bfloat16 [4096, 6144], P(None, ('expert', 'tensor')), may hold values from -0.09375 to 0.09375
- draft_down: bfloat16 [6144, 4096], P(('expert', 'tensor')), may hold values from -0.078125 to 0.078125
- final_gain: float32 [4096], replicated, may hold values from 0.5 to 1.5
Outputs:
- verified: bfloat16 [4, 320, 4096], P(None, ('groups', 'expert', 'tensor')), parts along dimension 1
- draft_out: bfloat16 [4, 64, 4096], P(None, ('groups', 'expert', 'tensor')), parts along dimension 1
There are 2 independent parts, one for each index of `groups`. A program takes and returns all parts, laid end to end along the dimension named above; an argument that names none is the same for every part. Nothing has to cross between parts.
Inputs may be any that keep to these rules, and one draw needn't show every extreme that they name: `expert_ids`: the 8 ids of a row differ. In each aligned block of 10 rows no expert is named by more than 5 rows, and in some block one expert is named by exactly 5 rows.
All inputs are finite; a program needn't handle non-finite values.
Results may differ from a plain program's by a relative error of at most 0.0068.
Values may be sent and summed in bfloat16 or wider, within the bound.
A program may use at most 128 MiB of HBM per device.

v0:
```python
import jax
import jax.numpy as jnp
from jax import lax
from jax.sharding import PartitionSpec as P

EPSILON = 1e-06
RING = ("expert", "tensor")


def rms_scale(values, weights):
    values = values.astype(jnp.float32)
    mean_square = jnp.mean(values * values, axis=-1, keepdims=True)
    return values * lax.rsqrt(mean_square + EPSILON) * weights


def local(
    hidden_rows,
    expert_ids,
    accepted,
    norm_gain,
    router,
    gate_weight,
    up_weight,
    down_weight,
    draft_gain,
    draft_gate,
    draft_up,
    draft_down,
    final_gain,
):
    rounds_total, rows_here, width = hidden_rows.shape
    expert_count = router.shape[1]
    requests_here = accepted.shape[1]
    draft_rows = rows_here // requests_here
    total = rounds_total * rows_here
    my_expert = lax.axis_index(RING)
    rows = hidden_rows.reshape(total, width).astype(jnp.float32)
    normed = rms_scale(rows, norm_gain).astype(jnp.bfloat16)
    logits = jnp.dot(normed, router, preferred_element_type=jnp.float32)
    ids = expert_ids.reshape(total, -1)
    named = jnp.any(ids[:, :, None] == jnp.arange(expert_count, dtype=jnp.int32), axis=1)
    weights = jnp.where(named, jnp.exp(logits), 0.0)
    table = weights / jnp.sum(weights, axis=1, keepdims=True)
    everyone = lax.all_gather(normed, RING, axis=0, tiled=True)
    table = lax.all_gather(table, RING, axis=0, tiled=True)
    share = jnp.sum(
        jnp.where(jnp.arange(expert_count) == my_expert, table, 0.0), axis=1, keepdims=True
    )
    gate_values = jnp.dot(everyone, gate_weight[0], preferred_element_type=jnp.float32)
    up_values = jnp.dot(everyone, up_weight[0], preferred_element_type=jnp.float32)
    active = (jax.nn.silu(gate_values) * up_values).astype(jnp.bfloat16)
    part = jnp.dot(active, down_weight[0], preferred_element_type=jnp.float32)
    part = (share * part).astype(jnp.bfloat16)
    mixed = lax.psum_scatter(part, RING, scatter_dimension=0, tiled=True)
    mixed = lax.psum(mixed, "sub").astype(jnp.float32)
    verified = (rows + mixed).astype(jnp.bfloat16)
    by_request = verified.reshape(rounds_total, requests_here, draft_rows, width)
    pick = jnp.arange(draft_rows, dtype=jnp.int32) == accepted[:, :, None]
    features = jnp.sum(jnp.where(pick[..., None], by_request.astype(jnp.float32), 0.0), axis=2)
    features = features.reshape(rounds_total * requests_here, width)
    draft_input = rms_scale(features, draft_gain).astype(jnp.bfloat16)
    pieces = lax.all_gather(draft_input, RING, axis=0, tiled=True)
    gate_part = jnp.dot(pieces, draft_gate, preferred_element_type=jnp.float32)
    up_part = jnp.dot(pieces, draft_up, preferred_element_type=jnp.float32)
    units = (jax.nn.silu(gate_part) * up_part).astype(jnp.bfloat16)
    summed = lax.psum_scatter(
        jnp.dot(units, draft_down, preferred_element_type=jnp.float32).astype(jnp.bfloat16),
        RING,
        scatter_dimension=0,
        tiled=True,
    ).astype(jnp.float32)
    draft_out = rms_scale(features + summed, final_gain).astype(jnp.bfloat16)
    return (
        verified.reshape(hidden_rows.shape),
        draft_out.reshape(rounds_total, requests_here, width),
    )


def solution(mesh):
    placed = (
        P(None, ("groups", "expert", "tensor"), None),
        P(None, ("groups", "expert", "tensor"), None),
        P(None, ("groups", "expert", "tensor")),
        P(),
        P(),
        P(("expert", "tensor"), None, "sub"),
        P(("expert", "tensor"), None, "sub"),
        P(("expert", "tensor"), "sub", None),
        P(),
        P(None, ("expert", "tensor")),
        P(None, ("expert", "tensor")),
        P(("expert", "tensor"), None),
        P(),
    )
    return jax.shard_map(
        local,
        mesh=mesh,
        in_specs=placed,
        out_specs=(
            P(None, ("groups", "expert", "tensor"), None),
            P(None, ("groups", "expert", "tensor"), None),
        ),
        check_vma=False,
    )
```

profile of v0, /device:TPU:0, one launch (start us, length us, event | category | flops | bytes accessed | tf_op | source)
XLA Modules:
  0.0 299.9 jit_solution(18209610796333644949)
XLA Ops:
  7.2 0.0 copy-start
  7.2 0.0 all-gather.4.cloned.1.call-start
  7.2 2.3 copy.37
  9.5 1.2 multiply_reduce_fusion
  10.8 2.2 reshape.74
  13.0 0.1 copy.43
  13.1 0.1 rsqrt.31
  13.1 1.9 multiply_convert_fusion.2
  15.1 0.0 all-gather.4.cloned.1.call-update
  15.1 0.0 reduce-scatter.3.cloned.1.call-start
  15.2 0.7 copy.38
  15.9 0.1 eq.40
  16.0 1.2 fusion.21
  17.2 24.0 %all-gather = f32[16,40,16]{1,2,0:T(8,128)S(1)} all-gather(f32[1,40,16]{1,2,0:T(8,128)S(1)} %divide_bitcast_fusion), channel_id=1, replica_groups=mesh['groups'=2,'expert'=4,'tensor'=4,'sub'=1] {'expert','tensor'}, dimensions={0}, use_global_device_ids=true | all-gather | bytes 43520 | tf_op jit(solution)/shard_map/all_gather | solution.py:45
  41.3 0.1 reshape.77
  41.4 0.1 select_reduce_fusion.1
  41.5 32.6 %all-gather.4.cloned.1.call-done = bf16[640,4096]{1,0:T(8,128)(2,1)} async-done(((bf16[40,4096]{1,0:T(8,128)(2,1)}), bf16[640,4096]{1,0:T(8,128)(2,1)}) %all-gather.4.cloned.1.call-update) | async-done | bytes 5242896 | tf_op jit(solution)/shard_map/all_gather | solution.py:44
  74.1 9.8 %fusion.3 = f32[640,768]{1,0:T(8,128)} fusion(bf16[640,4096]{1,0:T(8,128)(2,1)} %all-gather.4.cloned.1.call-done, bf16[1,4096,768]{2,1,0:T(8,128)(2,1)} %param.18), kind=kOutput, calls=%fused_computation.4 | convolution fusion | flops 4026531840 | bytes 13500416 | tf_op jit(solution)/shard_map/dot_general | solution.py:49
  83.9 18.5 %multiply_convert_fusion = bf16[640,4096]{1,0:T(8,128)(2,1)} fusion(bf16[1,768,4096]{2,1,0:T(8,128)(2,1)} %param.20, f32[640]{0:T(1024)S(1)} %select_reduce_fusion.1, f32[640,768]{1,0:T(8,128)} %fusion.3, bf16[640,4096]{1,0:T(8,128)(2,1)} %all-gather.4.cloned.1.call-done, bf16[1,4096,768]{2,1,0:T(8,128)(2,1)} %param.19), kind=kOutput, calls=%fused_computation | convolution fusion | flops 8061255680 | bytes 25037312 | tf_op jit(solution)/shard_map/dot_general | solution.py:52
  102.4 0.0 copy-start.3
  102.4 0.0 reduce-scatter.3.cloned.1.call-update
  102.4 0.0 all-gather.6.cloned.1.call-start
  102.4 0.6 copy-done.3
  103.0 0.1 copy.41
  103.1 0.1 iota_compare_fusion.1
  103.2 76.3 %reduce-scatter.3.cloned.1.call-done = bf16[40,4096]{1,0:T(8,128)(2,1)} async-done(((bf16[640,4096]{1,0:T(8,128)(2,1)}), bf16[40,4096]{1,0:T(8,128)(2,1)}) %reduce-scatter.3.cloned.1.call-update) | async-done | bytes 327696 | tf_op jit(solution)/shard_map/reduce_scatter | solution.py:54
  179.5 1.2 add_convert_fusion
  180.8 1.1 reshape.75
  181.9 2.4 select_reduce_fusion
  184.2 1.6 reshape.72
  185.9 1.1 multiply_reduce_fusion.2
  186.9 0.1 rsqrt.33
  187.0 0.0 copy-done.2
  187.0 1.6 multiply_convert_fusion.4
  188.6 0.0 all-gather.6.cloned.1.call-update
  188.7 0.2 reduce-scatter.5.cloned.1.call-start
  188.9 36.9 %all-gather.6.cloned.1.call-done = bf16[128,4096]{1,0:T(8,128)(2,1)} async-done(((bf16[8,4096]{1,0:T(8,128)(2,1)}), bf16[128,4096]{1,0:T(8,128)(2,1)}) %all-gather.6.cloned.1.call-update) | async-done | bytes 1048592 | tf_op jit(solution)/shard_map/all_gather | solution.py:62
  225.8 3.6 %fusion.22 = f32[128,384]{1,0:T(8,128)} fusion(bf16[128,4096]{1,0:T(8,128)(2,1)} %all-gather.6.cloned.1.call-done, bf16[4096,384]{1,0:T(8,128)(2,1)} %param.22), kind=kOutput, calls=%fused_computation.40 | convolution fusion | flops 402653184 | bytes 4390912 | tf_op jit(solution)/shard_map/dot_general | solution.py:63
  229.4 0.0 copy-done
  229.4 4.6 %convolution_convert_fusion = bf16[128,4096]{1,0:T(8,128)(2,1)} fusion(bf16[384,4096]{1,0:T(8,128)(2,1)S(1)} %copy-done, bf16[128,4096]{1,0:T(8,128)(2,1)} %all-gather.6.cloned.1.call-done, bf16[4096,384]{1,0:T(8,128)(2,1)} %param.23, f32[128,384]{1,0:T(8,128)} %fusion.22), kind=kOutput, calls=%fused_computation.6 | convolution fusion | flops 806125568 | bytes 8585216 | tf_op jit(solution)/shard_map/dot_general | solution.py:67
  234.0 0.0 reduce-scatter.5.cloned.1.call-update
  234.0 0.9 reshape.71
  234.9 2.0 copy.42
  237.0 53.7 %reduce-scatter.5.cloned.1.call-done = bf16[8,4096]{1,0:T(8,128)(2,1)} async-done(((bf16[128,4096]{1,0:T(8,128)(2,1)}), bf16[8,4096]{1,0:T(8,128)(2,1)}) %reduce-scatter.5.cloned.1.call-update) | async-done | bytes 65552 | tf_op jit(solution)/shard_map/reduce_scatter | solution.py:66
  290.7 1.1 multiply_reduce_fusion.1
  291.7 0.0 copy-done.1
  291.7 1.0 multiply_convert_fusion.3
  292.7 0.7 reshape.73
  (9 shorter events, 0.1 us)
Async XLA Ops:
  7.2 222.2 %copy-start = (bf16[384,4096]{1,0:T(8,128)(2,1)S(1)}, bf16[384,4096]{1,0:T(8,128)(2,1)}, u32[]{:S(2)}) copy-start(bf16[384,4096]{1,0:T(8,128)(2,1)} %param.24) | copy-start | bytes 9437188
  7.2 66.9 %all-gather.4.cloned.1.call-start = ((), (), s32[]{:S(2)}) async-start(), calls=%async_computation.2 | async-start | bytes 5570560 | tf_op jit(solution)/shard_map/all_gather | solution.py:44
  15.1 164.4 %reduce-scatter.3.cloned.1.call-start = ((), (), s32[]{:S(2)}) async-start(), calls=%async_computation.3 | async-start | bytes 5570560 | tf_op jit(solution)/shard_map/reduce_scatter | solution.py:54
  102.4 0.7 copy-start.3
  102.4 84.7 %copy-start.2 = (f32[4096]{0:T(1024)S(1)}, f32[4096]{0:T(1024)}, u32[]{:S(2)}) copy-start(f32[4096]{0:T(1024)} %param.21) | copy-start | bytes 49156
  102.4 123.4 %all-gather.6.cloned.1.call-start = ((), (), s32[]{:S(2)}) async-start(), calls=%async_computation.4 | async-start | bytes 1114112 | tf_op jit(solution)/shard_map/all_gather | solution.py:62
  188.7 102.0 %reduce-scatter.5.cloned.1.call-start = ((), (), s32[]{:S(2)}) async-start(), calls=%async_computation.5 | async-start | bytes 1114112 | tf_op jit(solution)/shard_map/reduce_scatter | solution.py:66
  229.4 62.3 %copy-start.1 = (f32[4096]{0:T(1024)S(1)}, f32[4096]{0:T(1024)}, u32[]{:S(2)}) copy-start(f32[4096]{0:T(1024)} %param.25) | copy-start | bytes 49156
Sparse Core Ops, SparseCore 0:
  15.2 58.7 all-gather.3
  102.5 76.9 reduce-scatter.2
  188.8 36.9 all-gather.5
  234.1 56.4 reduce-scatter.4
where the time goes:
time: 301 us; the launch traced here: 300 us
  waiting for transfers between devices  200 us (66%)
  matrix products  37.7 us (13%)
  blocking collectives  24 us (8%)
  between operations  13.8 us (5%)
  local copies, waits for them, and re-layouts  12.8 us (4%)
  other arithmetic  11.7 us (4%)
    reduce_scatter x1, waiting for transfers between devices, local(): mixed = lax.psum_scatter(part, RING, scatter_dimension=0, tiled=True)  76.3 us
    reduce_scatter x1, waiting for transfers between devices, local(): lax.psum_scatter(jnp.dot(units, draft_down, preferred_element_type=jnp.fl...  53.7 us
    all_gather x1, waiting for transfers between devices, local(): pieces = lax.all_gather(draft_input, RING, axis=0, tiled=True)  36.9 us
    all_gather x1, waiting for transfers between devices, local(): everyone = lax.all_gather(normed, RING, axis=0, tiled=True)  32.6 us
    all_gather x1, blocking collectives, local(): table = lax.all_gather(table, RING, axis=0, tiled=True)  24 us
    dot_general x1, matrix products, local(): part = jnp.dot(active, down_weight[0], preferred_element_type=jnp.float32)  18.5 us
    dot_general x1, matrix products, local(): jnp.dot(everyone, gate_weight[0], preferred_element_type=jnp.float32)  9.83 us
  transfers between devices with their start and end apart: 4, of which 4 were waited for; matrix products, arithmetic and copies ran while one was open for 2% of the time, Pallas kernels for 0%

commit v1 on v0

--- a/solution.py
+++ b/solution.py
@@ -41,8 +41,11 @@
     named = jnp.any(ids[:, :, None] == jnp.arange(expert_count, dtype=jnp.int32), axis=1)
     weights = jnp.where(named, jnp.exp(logits), 0.0)
     table = weights / jnp.sum(weights, axis=1, keepdims=True)
-    everyone = lax.all_gather(normed, RING, axis=0, tiled=True)
-    table = lax.all_gather(table, RING, axis=0, tiled=True)
+    everyone, table = jnp.split(
+        lax.all_gather(jnp.concatenate([normed, table], axis=1), RING, axis=0, tiled=True),
+        [normed.shape[1]],
+        axis=1,
+    )
     share = jnp.sum(
         jnp.where(jnp.arange(expert_count) == my_expert, table, 0.0), axis=1, keepdims=True
     )

time: 301 us -> 332 us (1.10)
  waiting for transfers between devices: 200 us -> 259 us
  blocking collectives: 24 us -> 0 us
  matrix products: 37.7 us -> 31.8 us
    all_gather x1, waiting for transfers between devices: 32.6 us -> 92.4 us  [local(): lax.all_gather(jnp.concatenate([normed, table], axis=1), RING, axis=0, ti...]
    all_gather x1 -> x0, blocking collectives: 24 us -> none  [local(): table = lax.all_gather(table, RING, axis=0, tiled=True)]
    dot_general x1, matrix products: 18.5 us -> 5.96 us  [local(): part = jnp.dot(active, down_weight[0], preferred_element_type=jnp.float32)]
    dot_general x0 -> x1, matrix products: none -> 7.34 us  [local(): jnp.dot(everyone, up_weight[0], preferred_element_type=jnp.float32)]
  transfers between devices with their start and end apart: 4 -> 4, of which waited for: 4 -> 4; matrix products, arithmetic and copies ran while one was open for 2% -> 1% of each run, Pallas kernels for 0% -> 0%
where the time goes in v1:
time: 332 us
  waiting for transfers between devices  259 us (78%)
  matrix products  31.8 us (10%)
  other arithmetic  13.9 us (4%)
  between operations  13.9 us (4%)
  local copies, waits for them, and re-layouts  12.7 us (4%)
    all_gather x1, waiting for transfers between devices, local(): lax.all_gather(jnp.concatenate([normed, table], axis=1), RING, axis=0, ti...  92.4 us
    reduce_scatter x1, waiting for transfers between devices, local(): mixed = lax.psum_scatter(part, RING, scatter_dimension=0, tiled=True)  75.9 us
    reduce_scatter x1, waiting for transfers between devices, local(): lax.psum_scatter(jnp.dot(units, draft_down, preferred_element_type=jnp.fl...  53.8 us
    all_gather x1, waiting for transfers between devices, local(): pieces = lax.all_gather(draft_input, RING, axis=0, tiled=True)  37.1 us
    dot_general x1, matrix products, local(): jnp.dot(everyone, gate_weight[0], preferred_element_type=jnp.float32)  8.91 us
    dot_general x1, matrix products, local(): jnp.dot(everyone, up_weight[0], preferred_element_type=jnp.float32)  7.34 us
  transfers between devices with their start and end apart: 4, of which 4 were waited for; matrix products, arithmetic and copies ran while one was open for 1% of the time, Pallas kernels for 0%

profile of v1, /device:TPU:0, one launch (start us, length us, event | category | flops | bytes accessed | tf_op | source)
XLA Modules:
  0.0 331.7 jit_solution(17097548730330170784)
XLA Ops:
  7.2 0.0 copy-start
  7.2 0.0 all-gather.3.cloned.1.call-start
  7.2 2.3 copy.38
  9.5 1.2 multiply_reduce_fusion
  10.8 2.1 reshape.74
  12.9 0.1 copy.44
  13.0 0.1 rsqrt.31
  13.1 0.7 copy.40
  13.8 0.1 eq.40
  13.9 2.1 fusion.22
  16.0 1.4 fusion.23
  17.4 0.1 copy.41
  17.5 2.0 pad_maximum_fusion
  19.5 0.0 all-gather.3.cloned.1.call-update
  19.5 0.0 reduce-scatter.3.cloned.1.call-start
  19.6 92.4 %all-gather.3.cloned.1.call-done = f32[640,4112]{1,0:T(8,128)} async-done(((f32[40,4112]{1,0:T(8,128)}), f32[640,4112]{1,0:T(8,128)}) %all-gather.3.cloned.1.call-update) | async-done | bytes 10526736 | tf_op jit(solution)/shard_map/all_gather | solution.py:45
  112.0 8.9 %fusion.2 = f32[640,768]{1,0:T(8,128)S(1)} fusion(f32[640,4112]{1,0:T(8,128)} %all-gather.3.cloned.1.call-done, bf16[1,4096,768]{2,1,0:T(8,128)(2,1)} %param.18), kind=kOutput, calls=%fused_computation.3 | convolution fusion | flops 4026531840 | bytes 13500416 | tf_op jit(solution)/shard_map/dot_general | solution.py:52
  120.9 0.0 copy-done.3
  120.9 0.2 fusion.13
  121.1 0.0 slice-start.1
  121.1 7.3 %multiply_convert_fusion.1 = bf16[640,768]{1,0:T(8,128)(2,1)S(1)} fusion(f32[640,768]{1,0:T(8,128)S(1)} %fusion.2, bf16[1,4096,768]{2,1,0:T(8,128)(2,1)} %param.19, f32[640,4112]{1,0:T(8,128)S(1)} %copy-done.3), kind=kOutput, calls=%fused_computation.9 | convolution fusion | flops 4029480960 | bytes 14483456 | tf_op jit(solution)/shard_map/dot_general | solution.py:53
  128.5 6.0 %multiply_convert_fusion = bf16[640,4096]{1,0:T(8,128)(2,1)} fusion(bf16[640,768]{1,0:T(8,128)(2,1)S(1)} %multiply_convert_fusion.1, bf16[1,768,4096]{2,1,0:T(8,128)(2,1)S(1)} %bitcast.21, f32[640]{0:T(1024)S(1)} %fusion.13), kind=kOutput, calls=%fused_computation | convolution fusion | flops 4031774720 | bytes 12519936 | tf_op jit(solution)/shard_map/dot_general | solution.py:55
  134.4 0.0 reduce-scatter.3.cloned.1.call-update
  134.5 0.0 all-gather.5.cloned.1.call-start
  134.5 0.6 copy-done.4
  135.1 0.1 copy.42
  135.2 0.1 iota_compare_fusion.1
  135.3 75.9 %reduce-scatter.3.cloned.1.call-done = bf16[40,4096]{1,0:T(8,128)(2,1)} async-done(((bf16[640,4096]{1,0:T(8,128)(2,1)}), bf16[40,4096]{1,0:T(8,128)(2,1)}) %reduce-scatter.3.cloned.1.call-update) | async-done | bytes 327696 | tf_op jit(solution)/shard_map/reduce_scatter | solution.py:57
  211.2 1.2 add_convert_fusion
  212.5 1.1 reshape.75
  213.6 2.4 select_reduce_fusion
  215.9 1.6 reshape.72
  217.6 1.1 multiply_reduce_fusion.2
  218.6 0.1 rsqrt.33
  218.7 0.0 copy-done.2
  218.7 1.6 multiply_convert_fusion.4
  220.3 0.0 all-gather.5.cloned.1.call-update
  220.4 0.0 reduce-scatter.5.cloned.1.call-start
  220.4 37.1 %all-gather.5.cloned.1.call-done = bf16[128,4096]{1,0:T(8,128)(2,1)} async-done(((bf16[8,4096]{1,0:T(8,128)(2,1)}), bf16[128,4096]{1,0:T(8,128)(2,1)}) %all-gather.5.cloned.1.call-update) | async-done | bytes 1048592 | tf_op jit(solution)/shard_map/all_gather | solution.py:65
  257.5 3.6 %fusion.24 = f32[128,384]{1,0:T(8,128)} fusion(bf16[128,4096]{1,0:T(8,128)(2,1)} %all-gather.5.cloned.1.call-done, bf16[4096,384]{1,0:T(8,128)(2,1)} %param.22), kind=kOutput, calls=%fused_computation.43 | convolution fusion | flops 402653184 | bytes 4390912 | tf_op jit(solution)/shard_map/dot_general | solution.py:66
  261.1 4.6 %convolution_convert_fusion = bf16[128,4096]{1,0:T(8,128)(2,1)} fusion(bf16[384,4096]{1,0:T(8,128)(2,1)S(1)} %copy-done, bf16[128,4096]{1,0:T(8,128)(2,1)} %all-gather.5.cloned.1.call-done, bf16[4096,384]{1,0:T(8,128)(2,1)} %param.23, f32[128,384]{1,0:T(8,128)} %fusion.24), kind=kOutput, calls=%fused_computation.8 | convolution fusion | flops 806125568 | bytes 8585216 | tf_op jit(solution)/shard_map/dot_general | solution.py:70
  265.7 0.0 reduce-scatter.5.cloned.1.call-update
  265.7 0.9 reshape.71
  266.6 2.0 copy.43
  268.7 53.8 %reduce-scatter.5.cloned.1.call-done = bf16[8,4096]{1,0:T(8,128)(2,1)} async-done(((bf16[128,4096]{1,0:T(8,128)(2,1)}), bf16[8,4096]{1,0:T(8,128)(2,1)}) %reduce-scatter.5.cloned.1.call-update) | async-done | bytes 65552 | tf_op jit(solution)/shard_map/reduce_scatter | solution.py:69
  322.4 1.1 multiply_reduce_fusion.1
  323.5 1.0 multiply_convert_fusion.3
  324.5 0.7 reshape.73
  (16 shorter events, 0.1 us)
Async XLA Ops:
  7.2 254.0 %copy-start = (bf16[384,4096]{1,0:T(8,128)(2,1)S(1)}, bf16[384,4096]{1,0:T(8,128)(2,1)}, u32[]{:S(2)}) copy-start(bf16[384,4096]{1,0:T(8,128)(2,1)} %param.24) | copy-start | bytes 9437188
  7.2 104.8 %all-gather.3.cloned.1.call-start = ((), (), s32[]{:S(2)}) async-start(), calls=%async_computation.2 | async-start | bytes 11489280 | tf_op jit(solution)/shard_map/all_gather | solution.py:45
  19.5 191.7 %reduce-scatter.3.cloned.1.call-start = ((), (), s32[]{:S(2)}) async-start(), calls=%async_computation.3 | async-start | bytes 5570560 | tf_op jit(solution)/shard_map/reduce_scatter | solution.py:57
  112.0 8.9 %copy-start.3 = (f32[640,4112]{1,0:T(8,128)S(1)}, f32[640,4112]{1,0:T(8,128)}, u32[]{:S(2)}) copy-start(f32[640,4112]{1,0:T(8,128)} %all-gather.3.cloned.1.call-done) | copy-start | bytes 31580164
  112.0 16.5 %slice-start = ((s8[6291456]{0:T(1024)(128)(4,1)}), s8[4194304]{0:T(1024)(128)(4,1)S(1)}, s32[]{:S(2)}) async-start(s8[6291456]{0:T(1024)(128)(4,1)} %bitcast.20), calls=%async_computation.6 | async-start | bytes 8388608
  121.1 7.4 %slice-start.1 = ((s8[6291456]{0:T(1024)(128)(4,1)}), s8[2097152]{0:T(1024)(128)(4,1)S(1)}, s32[]{:S(2)}) async-start(s8[6291456]{0:T(1024)(128)(4,1)} %bitcast.20), calls=%async_computation.7 | async-start | bytes 4194304
  134.4 0.7 copy-start.4
  134.4 84.3 %copy-start.2 = (f32[4096]{0:T(1024)S(1)}, f32[4096]{0:T(1024)}, u32[]{:S(2)}) copy-start(f32[4096]{0:T(1024)} %param.21) | copy-start | bytes 49156
  134.5 123.0 %all-gather.5.cloned.1.call-start = ((), (), s32[]{:S(2)}) async-start(), calls=%async_computation.4 | async-start | bytes 1114112 | tf_op jit(solution)/shard_map/all_gather | solution.py:65
  220.4 102.1 %reduce-scatter.5.cloned.1.call-start = ((), (), s32[]{:S(2)}) async-start(), calls=%async_computation.5 | async-start | bytes 1114112 | tf_op jit(solution)/shard_map/reduce_scatter | solution.py:69
  261.1 62.4 %copy-start.1 = (f32[4096]{0:T(1024)S(1)}, f32[4096]{0:T(1024)}, u32[]{:S(2)}) copy-start(f32[4096]{0:T(1024)} %param.25) | copy-start | bytes 49156
Sparse Core Ops, SparseCore 0:
  19.6 92.2 all-gather.2
  134.6 76.6 reduce-scatter.2
  220.5 36.9 all-gather.4
  265.8 56.5 reduce-scatter.4
